TPU v7x, 32 devices: a whole 2x2x4 slice. The times are simulated.
32 devices in a mesh: sector: 16 (over z, y, x), op: 2 (over core).
Axes of the slice: x: 2, y: 2, z: 4, core: 2. Of those that a mesh axis runs over, the one named last changes fastest.
Arguments:
- psi: bfloat16 [1024, 128, 128], P('sector'), may hold values from -6 to 6
- left_env: bfloat16 [2, 128, 128, 128], P('op', 'sector'), may hold values from -0.5 to 0.5
- right_env: bfloat16 [2, 128, 128, 128], P('op', 'sector'), may hold values from -0.375 to 0.375
- left_dims: int32 [128], replicated, may hold values from 64 to 128
- right_dims: int32 [128], replicated, may hold values from 64 to 128
- block_right: int32 [1024], replicated, may hold values from 0 to 127, as said below
Outputs:
- h_psi: bfloat16 [1024, 128, 128], P('sector', 'op')
Inputs may be any that keep to these rules, and one draw needn't show every extreme that they name: Block d * 64 + j lies in left sector d * 8 + j // 8; its right sector is owned by index block_right // 8 of sector, and block_right % 8 equals j // 8. Of the 64 blocks of each index of sector, exactly 4 have their right sector owned by each index of sector; the 8 blocks of one left sector have distinct right sectors, and every right sector is paired with exactly 8 blocks.
All inputs are finite; a program needn't handle non-finite values.
Results may differ from a plain program's by a relative error of at most 0.0049.
Values may be sent and summed in bfloat16 or wider, within the bound.
A program may use at most 64 MiB of HBM per device.

v0:
```python
import jax
import jax.numpy as jnp
from jax import lax
from jax.sharding import PartitionSpec as P


def combine(partial_sum):
    row_count = partial_sum.shape[1] // lax.axis_size("op")
    whole = lax.psum(partial_sum, "op")
    return lax.dynamic_slice_in_dim(whole, lax.axis_index("op") * row_count, row_count, 1)


def per_device(psi, left_env, right_env, left_dims, right_dims, block_right):
    devices = lax.axis_size("sector")
    sector_index = lax.axis_index("sector")
    blocks = psi.shape[0]
    block_width = psi.shape[1]
    term_count = left_env.shape[0]
    sectors = left_env.shape[1]
    coupled = blocks // sectors
    slot_count = blocks // devices
    counter = jnp.arange(blocks, dtype=jnp.int32)
    mine_right = lax.dynamic_slice_in_dim(block_right, sector_index * blocks, blocks)
    mine_owner = mine_right // sectors
    send_order = jnp.argsort(mine_owner * blocks + counter)
    inverse = jnp.argsort(send_order)
    own_dims = lax.dynamic_slice_in_dim(left_dims, sector_index * sectors, sectors)
    row_limit = jnp.repeat(own_dims, coupled)
    col_limit = right_dims[mine_right]
    position = jnp.arange(block_width, dtype=jnp.int32)
    keep_mask = (position[None, :, None] < row_limit[:, None, None]) & (
        position[None, None, :] < col_limit[:, None, None]
    )
    masked = psi * keep_mask.astype(psi.dtype)
    products = jnp.einsum(
        "ksab,snbc->ksnac",
        left_env,
        masked.reshape(sectors, coupled, block_width, block_width),
        preferred_element_type=jnp.float32,
    )
    products = products.astype(jnp.bfloat16).reshape(term_count, blocks, block_width, block_width)
    owners_all = (block_right // sectors).reshape(devices, blocks)
    foreign = (owners_all != sector_index).astype(jnp.int32)
    incoming = jnp.argsort(foreign * blocks + counter[None, :], axis=1)[:, :slot_count]
    arriving = (
        jnp.take_along_axis(block_right.reshape(devices, blocks), incoming, axis=1).reshape(-1)
        - sector_index * sectors
    )
    outgoing = right_env[:, arriving].reshape(
        term_count, devices, slot_count, block_width, block_width
    )
    received = lax.all_to_all(outgoing, "sector", split_axis=1, concat_axis=1, tiled=True)
    chosen = received.reshape(term_count, blocks, block_width, block_width)[:, inverse]
    partial_sum = jnp.einsum("kjab,kjcb->jac", products, chosen, preferred_element_type=jnp.float32)
    result = combine(partial_sum).astype(jnp.bfloat16)
    row_count = result.shape[1]
    op_index = lax.axis_index("op")
    row_position = op_index * row_count + jnp.arange(row_count, dtype=jnp.int32)
    keep_rows = (row_position[None, :, None] < row_limit[:, None, None]) & (
        position[None, None, :] < col_limit[:, None, None]
    )
    return result * keep_rows.astype(jnp.bfloat16)


def solution(mesh):
    in_specs = (
        P("sector", None, None),
        P("op", "sector", None, None),
        P("op", "sector", None, None),
        P(),
        P(),
        P(),
    )
    out_specs = P("sector", "op", None)
    return jax.shard_map(
        per_device, mesh=mesh, in_specs=in_specs, out_specs=out_specs, check_vma=False
    )
```

profile of v0, /device:TPU:13, one launch (start us, length us, event | category | flops | bytes accessed | tf_op | source)
XLA Modules:
  0.0 86.6 jit_solution(15736413275250530421)
XLA Ops:
  0.0 0.0 copy-start
  0.0 0.8 reshape.167
  0.8 0.7 fusion.4
  1.5 0.1 mul.34
  1.6 0.1 copy.23
  1.7 1.0 %sort.48 = (s32[16,64]{0,1:T(8,128)}, s32[16,64]{0,1:T(8,128)S(1)}) sort(s32[16,64]{0,1:T(8,128)S(1)} %iota_add_fusion, s32[16,64]{0,1:T(8,128)S(1)} %iota.41), dimensions={1}, to_apply=%region_0.1 | sort | flops 10240 | bytes 16384 | tf_op jit(solution)/shard_map/jit(argsort)/sort | solution.py:44
  2.7 0.1 copy.24
  2.8 0.1 reshape.200
  2.9 0.8 gather_fusion.3
  3.7 0.1 reshape.203
  3.8 0.1 copy.25
  3.9 0.1 copy.26
  4.0 0.1 sub.31
  4.1 0.0 copy-done
  4.1 2.2 %gather_fusion.1 = bf16[64,128,128]{2,1,0:T(8,128)(2,1)} fusion(bf16[8,128,128]{2,1,0:T(8,128)(2,1)S(1)} %bitcast.24, s32[1024]{0:T(1024)S(1)} %pad_clamp_fusion.1), kind=kCustom, calls=%fused_computation.1 | custom fusion | bytes 4194560 | tf_op jit(solution)/shard_map/gather | solution.py:49
  6.3 0.0 copy-start.3
  6.3 0.0 copy-start.1
  6.3 6.7 %all-to-all-start = ((bf16[1,16,4,128,128]{4,3,2,0,1:T(8,128)(2,1)}), bf16[1,16,4,128,128]{4,3,2,0,1:T(8,128)(2,1)S(1)}, u32[]{:S(2)}, u32[]{:S(2)}) async-start(bf16[1,16,4,128,128]{4,3,2,0,1:T(8,128)(2,1)} %bitcast.26), calls=%async_computation | async-start | bytes 4194304 | tf_op jit(solution)/shard_map/all_to_all | solution.py:52
  13.0 0.0 copy-done.3
  13.0 0.1 dynamic_slice.9
  13.1 0.1 broadcast_in_dim.10
  13.2 0.1 lt.98
  13.2 0.8 iota_add_fusion.1
  14.0 0.0 copy-done.1
  14.0 0.8 gather_fusion
  14.8 2.0 %sort.49 = (s32[64]{0:T(128)}, s32[64]{0:T(128)S(1)}) sort(s32[64]{0:T(128)S(1)} %get-tuple-element.11, s32[64]{0:T(128)S(1)} %iota.43), dimensions={0}, to_apply=%region_1.2 | sort | flops 384 | bytes 1024 | tf_op jit(solution)/shard_map/jit(argsort)/sort | solution.py:25
  16.9 2.0 %sort.50 = (s32[64]{0:T(128)}, s32[64]{0:T(128)S(1)}) sort(s32[64]{0:T(128)S(1)} %get-tuple-element.9, s32[64]{0:T(128)S(1)} %iota.44), dimensions={0}, to_apply=%region_2.3 | sort | flops 384 | bytes 1024 | tf_op jit(solution)/shard_map/jit(argsort)/sort | solution.py:26
  18.9 0.1 broadcast_compare_fusion
  19.0 0.1 iota_compare_fusion
  19.1 0.0 copy-start.2
  19.1 3.2 %and_select_fusion = bf16[64,128,128]{2,1,0:T(8,128)(2,1)S(1)} fusion(bf16[64,128,128]{2,1,0:T(8,128)(2,1)} %param.6, pred[64,128]{1,0:T(8,128)(4,1)S(1)} %get-tuple-element.14, pred[64,128]{1,0:T(8,128)(4,1)S(1)} %get-tuple-element.13), kind=kLoop, calls=%fused_computation.4 | loop fusion | flops 2097152 | bytes 4210688 | tf_op jit(solution)/shard_map/mul | solution.py:34
  22.3 0.0 copy-done.2
  22.3 2.1 %convolution_convert_fusion = bf16[8,8,128,128]{3,2,1,0:T(8,128)(2,1)} fusion(bf16[8,8,128,128]{3,2,1,0:T(8,128)(2,1)S(1)} %bitcast.27, bf16[1,8,128,128]{3,2,1,0:T(8,128)(2,1)S(1)} %copy-done.2), kind=kOutput, calls=%fused_computation.7 | convolution fusion | flops 269484032 | bytes 4456448 | tf_op jit(solution)/shard_map/ksab,snbc->ksnac/dot_general | solution.py:35
  24.5 36.5 %all-to-all-done = bf16[1,16,4,128,128]{4,3,2,0,1:T(8,128)(2,1)S(1)} async-done(((bf16[1,16,4,128,128]{4,3,2,0,1:T(8,128)(2,1)}), bf16[1,16,4,128,128]{4,3,2,0,1:T(8,128)(2,1)S(1)}, u32[]{:S(2)}, u32[]{:S(2)}) %all-to-all-start) | async-done | bytes 2097184 | tf_op jit(solution)/shard_map/all_to_all | solution.py:52
  61.0 2.2 %gather_fusion.2 = bf16[64,128,128]{2,1,0:T(8,128)(2,1)} fusion(bf16[64,128,128]{2,1,0:T(8,128)(2,1)S(1)} %bitcast.25, s32[1024]{0:T(1024)S(1)} %pad_clamp_fusion), kind=kCustom, calls=%fused_computation.2 | custom fusion | bytes 4194560 | tf_op jit(solution)/shard_map/gather | solution.py:53
  63.1 5.8 %fusion.6 = f32[64,128,128]{2,1,0:T(8,128)} fusion(bf16[64,128,128]{1,2,0:T(8,128)(2,1)} %bitcast.28, bf16[64,128,128]{2,1,0:T(8,128)(2,1)} %gather_fusion.2), kind=kOutput, calls=%fused_computation.38 | convolution fusion | flops 268435456 | bytes 8388608 | tf_op jit(solution)/shard_map/kjab,kjcb->jac/dot_general | solution.py:54
  68.9 16.2 %all-reduce.1 = bf16[64,128,128]{2,1,0:T(8,128)(2,1)S(1)} all-reduce(f32[64,128,128]{2,1,0:T(8,128)} %fusion.6), channel_id=1, replica_groups=mesh['sector'=16,'op'=2] {'op'}, use_global_device_ids=true, to_apply=%region_3.4 | all-reduce | flops 1048576 | bytes 6291456 | tf_op jit(solution)/shard_map/psum | solution.py:9
  85.1 1.5 %and_select_fusion.1 = bf16[64,64,128]{2,1,0:T(8,128)(2,1)} fusion(bf16[64,128,128]{2,1,0:T(8,128)(2,1)S(1)} %all-reduce.1, s32[]{:T(128)S(6)} %select_n.61, pred[64,128]{1,0:T(8,128)(4,1)S(1)} %get-tuple-element.14, pred[64,64]{1,0:T(8,128)(4,1)S(1)} %broadcast_compare_fusion), kind=kLoop, calls=%fused_computation.6 | loop fusion | flops 1048576 | bytes 2109444 | tf_op jit(solution)/shard_map/mul | solution.py:62
  (12 shorter events, 0.1 us)
Async XLA Ops:
  0.0 4.1 %copy-start = (bf16[1,8,128,128]{3,2,1,0:T(8,128)(2,1)S(1)}, bf16[1,8,128,128]{3,2,1,0:T(8,128)(2,1)}, u32[]{:S(2)}) copy-start(bf16[1,8,128,128]{3,2,1,0:T(8,128)(2,1)} %param.8) | copy-start | bytes 786436
  6.3 6.7 %copy-start.3 = (s32[128]{0:T(128)S(1)}, s32[128]{0:T(128)}, u32[]{:S(2)}) copy-start(s32[128]{0:T(128)} %param.9) | copy-start | bytes 1540
  6.3 7.8 %copy-start.1 = (s32[128]{0:T(128)S(1)}, s32[128]{0:T(128)}, u32[]{:S(2)}) copy-start(s32[128]{0:T(128)} %param.10) | copy-start | bytes 1540
  6.3 54.7 %all-to-all-start = ((bf16[1,16,4,128,128]{4,3,2,0,1:T(8,128)(2,1)}), bf16[1,16,4,128,128]{4,3,2,0,1:T(8,128)(2,1)S(1)}, u32[]{:S(2)}, u32[]{:S(2)}) async-start(bf16[1,16,4,128,128]{4,3,2,0,1:T(8,128)(2,1)} %bitcast.26), calls=%async_computation | async-start | bytes 4194304 | tf_op jit(solution)/shard_map/all_to_all | solution.py:52
  19.1 3.2 %copy-start.2 = (bf16[1,8,128,128]{3,2,1,0:T(8,128)(2,1)S(1)}, bf16[1,8,128,128]{3,2,1,0:T(8,128)(2,1)}, u32[]{:S(2)}) copy-start(bf16[1,8,128,128]{3,2,1,0:T(8,128)(2,1)} %param.7) | copy-start | bytes 786436
where the time goes:
time: 86.9 us; the launch traced here: 86.6 us
  waiting for transfers between devices  36.5 us (42%)
  blocking collectives  16.2 us (19%)
  other arithmetic  11.5 us (13%)
  matrix products  7.91 us (9%)
  local copies, waits for them, and re-layouts  7.65 us (9%)
  starting transfers between devices  6.74 us (8%)
    all_to_all x1, waiting for transfers between devices, per_device(): lax.all_to_all(outgoing, 'sector', split_axis=1, concat_axis=1, tiled=True)  36.5 us
    psum x1, blocking collectives, combine(): whole = lax.psum(partial_sum, 'op')  16.2 us
    all_to_all x1, starting transfers between devices, per_device(): lax.all_to_all(outgoing, 'sector', split_axis=1, concat_axis=1, tiled=True)  6.74 us
    dot_general x1, matrix products, per_device(): jnp.einsum('kjab,kjcb->jac', products, chosen, preferred_element_type=jnp...  5.76 us
    mul x1, other arithmetic, per_device(): masked = psi * keep_mask.astype(psi.dtype)  3.23 us
    gather x1, local copies, waits for them, and re-layouts, per_device(): right_env[:, arriving]  2.17 us
    gather x1, local copies, waits for them, and re-layouts, per_device(): received.reshape(term_count, blocks, block_width, block_width)[:, inverse]  2.16 us
    dot_general x1, matrix products, per_device(): jnp.einsum('ksab,snbc->ksnac', left_env, masked.reshape(sectors, coupled,...  2.15 us
  transfers between devices with their start and end apart: 1, of which 1 were waited for; matrix products, arithmetic and copies ran while one was open for 13% of the time, Pallas kernels for 0%

commit v1 on v0

--- a/solution.py
+++ b/solution.py
@@ -1,8 +1,13 @@
+import functools
+
 import jax
 import jax.numpy as jnp
 from jax import lax
+from jax.experimental import pallas as pl
+from jax.experimental.pallas import tpu as pltpu
 from jax.sharding import PartitionSpec as P
 
+MESH = pl.DeviceIdType.MESH
 
 def combine(partial_sum):
     row_count = partial_sum.shape[1] // lax.axis_size("op")
@@ -10,7 +15,7 @@
     return lax.dynamic_slice_in_dim(whole, lax.axis_index("op") * row_count, row_count, 1)
 
 
-def per_device(psi, left_env, right_env, left_dims, right_dims, block_right):
+def exchange_path(psi, left_env, right_env, left_dims, right_dims, block_right):
     devices = lax.axis_size("sector")
     sector_index = lax.axis_index("sector")
     blocks = psi.shape[0]
@@ -62,6 +67,250 @@
     return result * keep_rows.astype(jnp.bfloat16)
 
 
+def gather_kernel(
+    devices, block_right, left_dims, right_dims, rank, source, psi_hbm, left_hbm, right_hbm, out,
+    psi, left, products, full, stage, got, part, partner_part,
+    local_sem, own_sem, z_send, z_recv, n_send, n_recv, s_send, s_recv, p_send, p_recv,
+):
+    me = lax.axis_index("sector")
+    core = lax.axis_index("op")
+    depth = devices // 4
+    z, y, x = me // 4, (me // 2) % 2, me % 2
+    x_mate, y_mate = me + 1 - 2 * x, me + 2 - 4 * y
+    blocks, width = psi.shape[0], psi.shape[1]
+    sectors = left.shape[0]
+    coupled = blocks // sectors
+    slots = blocks // devices
+    half = width // 2
+    place = (y, x)
+    near = (y_mate, x_mate)
+    far = (x_mate, y_mate)
+
+    own = [
+        pltpu.make_async_copy(
+            right_hbm.at[0, :, pl.ds(h * half, half), :], full.at[h, z, place[h]], own_sem.at[h]
+        )
+        for h in (0, 1)
+    ]
+    load_left = pltpu.make_async_copy(left_hbm.at[0], left, local_sem.at[0])
+    load_psi = pltpu.make_async_copy(psi_hbm, psi, local_sem.at[1])
+    for copy in (*own, load_left, load_psi):
+        copy.start()
+
+    barrier = pltpu.get_barrier_semaphore()
+    for mate in (x_mate, y_mate):
+        pl.semaphore_signal(barrier, inc=1, device_id={"sector": mate}, device_id_type=MESH)
+    pl.semaphore_signal(barrier, inc=1, device_id={"op": 1 - core}, device_id_type=MESH)
+
+    @pl.when(z > 0)
+    def _():
+        pl.semaphore_signal(barrier, inc=1, device_id={"sector": me - 4}, device_id_type=MESH)
+
+    @pl.when(z < depth - 1)
+    def _():
+        pl.semaphore_signal(barrier, inc=1, device_id={"sector": me + 4}, device_id_type=MESH)
+
+    pl.semaphore_wait(barrier, 3 + (z > 0).astype(jnp.int32) + (z < depth - 1).astype(jnp.int32))
+    for copy in own:
+        copy.wait()
+
+    def remote(src, dst, send, recv, target):
+        return pltpu.make_async_remote_copy(
+            src_ref=src, dst_ref=dst, send_sem=send, recv_sem=recv, device_id=target, device_id_type=MESH
+        )
+
+    def along_z(h, zz, up):
+        block = full.at[h, zz, place[h]]
+        target = {"sector": me + 4 if up else me - 4}
+        return remote(block, block, z_send.at[h, zz, int(up)], z_recv.at[h, zz], target)
+
+    def to_near(h, zz):
+        block = full.at[h, zz, place[h]]
+        return remote(block, block, n_send.at[h, zz], n_recv.at[h, zz], {"sector": near[h]})
+
+    def to_far(h, zz, p):
+        return remote(
+            stage.at[h, zz, p], got.at[h, zz, p], s_send.at[h, zz, p], s_recv.at[h, zz, p], {"sector": far[h]}
+        )
+
+    def select_and_send(h, zz, p):
+        owner = (zz * 2 + p) * 2 + x if h == 0 else (zz * 2 + y) * 2 + p
+        for t in range(slots):
+            wanted = source[(h * devices + owner) * slots + t]
+            value = full[h, zz, p, 0]
+            for s in range(1, sectors):
+                value = jnp.where(wanted == s, full[h, zz, p, s], value)
+            stage[h, zz, p, t] = value
+        to_far(h, zz, p).start()
+
+    def arrived(zz, ups):
+        for h in (0, 1):
+            for up in ups:
+                @pl.when(z < depth - 1 if up else z > 0)
+                def _():
+                    along_z(h, zz, up).start()
+            to_near(h, zz).start()
+        for h in (0, 1):
+            select_and_send(h, zz, place[h])
+
+    def near_arrived(zz):
+        for h in (0, 1):
+            to_near(h, zz).wait_recv()
+            select_and_send(h, zz, 1 - place[h])
+
+    columns = lax.broadcasted_iota(jnp.int32, (width, width), 1)
+
+    def multiply_left(s, _):
+        row_limit = left_dims[me * sectors + s]
+        env = jnp.where(columns < row_limit, left[s].astype(jnp.float32), 0.0).astype(jnp.bfloat16)
+        for n in range(coupled):
+            j = s * coupled + n
+            col_limit = right_dims[block_right[me * blocks + j]]
+            value = jnp.dot(env, psi[j], preferred_element_type=jnp.float32)
+            products[j] = jnp.where(columns < col_limit, value, 0.0).astype(jnp.bfloat16)
+        return 0
+
+    arrived(z, (False, True))
+    load_left.wait()
+    load_psi.wait()
+    lax.fori_loop(0, sectors // 2, multiply_left, 0)
+    near_arrived(z)
+    for step in range(1, depth):
+        below, above = z - step, z + step
+
+        def enter(zz, up):
+            for h in (0, 1):
+                along_z(h, zz, up).wait_recv()
+            arrived(zz, (up,))
+
+        pl.when(below >= 0)(functools.partial(enter, below, True))
+        pl.when(above < depth)(functools.partial(enter, above, False))
+        if step == 1:
+            lax.fori_loop(sectors // 2, sectors, multiply_left, 0)
+        pl.when(below >= 0)(functools.partial(near_arrived, below))
+        pl.when(above < depth)(functools.partial(near_arrived, above))
+    for h in (0, 1):
+        for zz in range(depth):
+            for p in (0, 1):
+                to_far(h, zz, p).wait_recv()
+
+    def swap(s):
+        span = pl.ds(s * coupled, coupled)
+        return remote(
+            part.at[1 - core, span], partner_part.at[span], p_send.at[s], p_recv.at[s], {"op": 1 - core}
+        )
+
+    def multiply_right(s, _):
+        for n in range(coupled):
+            j = s * coupled + n
+            owner = block_right[me * blocks + j] // sectors
+            oz, oy, ox = owner // 4, (owner // 2) % 2, owner % 2
+            slot = rank[j]
+            top = jnp.where(ox == x, full[0, oz, oy, s], got[0, oz, oy, slot])
+            low = jnp.where(oy == y, full[1, oz, ox, s], got[1, oz, ox, slot])
+            env = jnp.concatenate([top, low], axis=0)
+            value = lax.dot_general(
+                products[j], env, (((1,), (1,)), ((), ())), preferred_element_type=jnp.float32
+            )
+            part[0, j] = value[:half].astype(part.dtype)
+            part[1, j] = value[half:].astype(part.dtype)
+        swap(s).start()
+        return 0
+
+    def finish(s):
+        swap(s).wait_recv()
+        rows = lax.broadcasted_iota(jnp.int32, (half, width), 0) + core * half
+        row_limit = left_dims[me * sectors + s]
+        for n in range(coupled):
+            j = s * coupled + n
+            col_limit = right_dims[block_right[me * blocks + j]]
+            value = part[core, j].astype(jnp.float32) + partner_part[j].astype(jnp.float32)
+            keep = (rows < row_limit) & (columns[:half] < col_limit)
+            out[j] = jnp.where(keep, value, 0.0).astype(jnp.bfloat16)
+
+    lag = 2
+    lax.fori_loop(0, lag, multiply_right, 0)
+
+    def both(s, _):
+        multiply_right(s, 0)
+        finish(s - lag)
+        return 0
+
+    lax.fori_loop(lag, sectors, both, 0)
+
+    def last(s, _):
+        finish(s)
+        return 0
+
+    lax.fori_loop(sectors - lag, sectors, last, 0)
+
+    def drain(s, _):
+        swap(s).wait_send()
+        return 0
+
+    lax.fori_loop(0, sectors, drain, 0)
+    for h in (0, 1):
+        for zz in range(depth):
+            to_near(h, zz).wait_send()
+            for p in (0, 1):
+                to_far(h, zz, p).wait_send()
+            pl.when((z > 0) & (z <= zz))(lambda: along_z(h, zz, False).wait_send())
+            pl.when((z < depth - 1) & (z >= zz))(lambda: along_z(h, zz, True).wait_send())
+
+
+def tables(block_right, devices, blocks, sectors):
+    me = lax.axis_index("sector")
+    slots = blocks // devices
+    members = jnp.stack([me, me ^ 1, me ^ 2])
+    owners = (block_right.reshape(devices, blocks) // sectors)[members]
+    position = jnp.arange(blocks, dtype=jnp.int32)
+    earlier = (owners[:, None, :] == owners[:, :, None]) & (position[None, None, :] < position[None, :, None])
+    rank = jnp.sum(earlier.astype(jnp.int32), axis=2)
+    code = owners[1:] * slots + rank[1:]
+    hit = code[:, None, :] == jnp.arange(devices * slots, dtype=jnp.int32)[None, :, None]
+    source = jnp.sum(hit * (position // (blocks // sectors)), axis=2)
+    return rank[0], source.reshape(-1)
+
+
+def per_device(psi, left_env, right_env, left_dims, right_dims, block_right):
+    devices, cores = lax.axis_size("sector"), lax.axis_size("op")
+    blocks, width = psi.shape[0], psi.shape[1]
+    terms, sectors = left_env.shape[0], left_env.shape[1]
+    if cores != 2 or devices % 4 or terms != 1 or blocks % devices or blocks // devices > sectors:
+        return exchange_path(psi, left_env, right_env, left_dims, right_dims, block_right)
+    depth, half, slots = devices // 4, width // 2, blocks // devices
+    rank, source = tables(block_right, devices, blocks, sectors)
+    smem, anywhere = pl.BlockSpec(memory_space=pltpu.SMEM), pl.BlockSpec(memory_space=pl.ANY)
+    dma, bf16 = pltpu.SemaphoreType.DMA, jnp.bfloat16
+    return pl.pallas_call(
+        functools.partial(gather_kernel, devices),
+        out_shape=jax.ShapeDtypeStruct((blocks, half, width), bf16),
+        in_specs=[smem] * 5 + [anywhere] * 3,
+        out_specs=pl.BlockSpec(memory_space=pltpu.VMEM),
+        scratch_shapes=[
+            pltpu.VMEM((blocks, width, width), bf16),
+            pltpu.VMEM((sectors, width, width), bf16),
+            pltpu.VMEM((blocks, width, width), bf16),
+            pltpu.VMEM((2, depth, 2, sectors, half, width), bf16),
+            pltpu.VMEM((2, depth, 2, slots, half, width), bf16),
+            pltpu.VMEM((2, depth, 2, slots, half, width), bf16),
+            pltpu.VMEM((2, blocks, half, width), jnp.float32),
+            pltpu.VMEM((blocks, half, width), jnp.float32),
+            dma((2,)),
+            dma((2,)),
+            dma((2, depth, 2)),
+            dma((2, depth)),
+            dma((2, depth)),
+            dma((2, depth)),
+            dma((2, depth, 2)),
+            dma((2, depth, 2)),
+            dma((sectors,)),
+            dma((sectors,)),
+        ],
+        compiler_params=pltpu.CompilerParams(collective_id=0, has_side_effects=True),
+    )(block_right, left_dims, right_dims, rank, source, psi, left_env, right_env)
+
+
 def solution(mesh):
     in_specs = (
         P("sector", None, None),

time: 86.9 us -> 47.8 us (0.55)
  the two profiles are of different devices: /device:TPU:13 before, /device:TPU:1 now
where the time goes in v1:
time: 47.8 us; the launch traced here: 47.6 us
  Pallas kernels  42.3 us (88%)
  local copies, waits for them, and re-layouts  4.77 us (10%)
    pallas_call x1, Pallas kernels, per_device(): pl.pallas_call(functools.partial(gather_kernel, devices), out_shape=jax.S...  42.3 us
    unnamed x1, local copies, waits for them, and re-layouts  2.26 us

profile of v1, /device:TPU:1, one launch (start us, length us, event | category | flops | bytes accessed | tf_op | source)
XLA Modules:
  0.0 47.6 jit_solution(2732360629450216400)
XLA Ops:
  0.0 0.1 fusion.2
  0.1 0.8 %reshape.160 = s32[16,64]{1,0:T(8,128)S(1)} reshape(s32[1024]{0:T(1024)} %block_right.1) | data formatting | bytes 8192 | tf_op jit(solution)/shard_map/reshape | solution.py:265
  0.9 0.6 %gather_fusion = s32[3,64]{1,0:T(4,128)S(1)} fusion(s32[16,64]{1,0:T(8,128)S(1)} %add_select_fusion, s32[1024]{0:T(1024)S(1)} %pad_clamp_fusion), kind=kCustom, calls=%fused_computation | custom fusion | bytes 1548 | tf_op jit(solution)/shard_map/gather | solution.py:265
  1.4 0.2 convert_reduce_fusion
  1.7 0.5 %slice_bitcast_fusion.rank = s32[64]{0:T(128)} fusion(s32[3,64]{1,0:T(4,128)S(1)} %convert_reduce_fusion), kind=kLoop, calls=%fused_computation.20 | loop fusion | bytes 512 | tf_op jit(solution)/shard_map/squeeze | solution.py:272
  2.2 0.1 select_reduce_fusion
  2.3 0.7 %reshape.161.source = s32[128]{0:T(128)} reshape(s32[2,64]{1,0:T(2,128)S(1)} %select_reduce_fusion) | data formatting | bytes 1024 | tf_op jit(solution)/shard_map/reshape | solution.py:272
  3.0 42.3 %shard_map.64 = bf16[64,64,128]{2,1,0:T(8,128)(2,1)} custom-call(s32[1024]{0:T(1024)} %block_right.1, s32[128]{0:T(128)} %left_dims.1, s32[128]{0:T(128)} %right_dims.1, s32[64]{0:T(128)} %slice_bitcast_fusion.rank, s32[128]{0:T(128)} %reshape.161.source, bf16[64,128,128]{2,1,0:T(8,128)(2,1)} %psi_hbm.1, bf16[1,8,128,128]{3,2,1,0:T(8,128)(2,1)} %left_hbm.1, ...), custom_call_target="tpu_custom_call" | custom-call | tf_op jit(solution)/shard_map/pallas_call | solution.py:285
  45.3 2.3 %copy.8 = bf16[64,64,128]{2,1,0:T(8,128)(2,1)} copy(bf16[64,64,128]{2,1,0:T(8,128)(2,1)} %shard_map.64) | data formatting | bytes 2097152
  (5 shorter events, 0.0 us)

commit v2 on v1

--- a/solution.py
+++ b/solution.py
@@ -136,7 +136,7 @@
     def select_and_send(h, zz, p):
         owner = (zz * 2 + p) * 2 + x if h == 0 else (zz * 2 + y) * 2 + p
         for t in range(slots):
-            wanted = source[(h * devices + owner) * slots + t]
+            wanted = source[far[h], owner * slots + t] // coupled
             value = full[h, zz, p, 0]
             for s in range(1, sectors):
                 value = jnp.where(wanted == s, full[h, zz, p, s], value)
@@ -170,6 +170,39 @@
             products[j] = jnp.where(columns < col_limit, value, 0.0).astype(jnp.bfloat16)
         return 0
 
+    def swap(zz):
+        return remote(
+            part.at[1 - core, zz], partner_part.at[zz], p_send.at[zz], p_recv.at[zz], {"op": 1 - core}
+        )
+
+    def pick(h, zz, p, wanted):
+        value = full[h, zz, p, 0]
+        for s in range(1, sectors):
+            value = jnp.where(wanted == s, full[h, zz, p, s], value)
+        return value
+
+    def multiply_right(zz):
+        for h in (0, 1):
+            for p in (0, 1):
+                to_far(h, zz, p).wait_recv()
+
+        def one(i, _):
+            oy, ox, slot = i // (2 * slots), (i // slots) % 2, i % slots
+            j = source[me, (zz * 4 + oy * 2 + ox) * slots + slot]
+            wanted = j // coupled
+            top = jnp.where(ox == x, pick(0, zz, oy, wanted), got[0, zz, oy, slot])
+            low = jnp.where(oy == y, pick(1, zz, ox, wanted), got[1, zz, ox, slot])
+            env = jnp.concatenate([top, low], axis=0)
+            value = lax.dot_general(
+                products[j], env, (((1,), (1,)), ((), ())), preferred_element_type=jnp.float32
+            )
+            part[0, zz, i] = value[:half]
+            part[1, zz, i] = value[half:]
+            return 0
+
+        lax.fori_loop(0, 4 * slots, one, 0, unroll=4)
+        swap(zz).start()
+
     arrived(z, (False, True))
     load_left.wait()
     load_psi.wait()
@@ -189,66 +222,31 @@
             lax.fori_loop(sectors // 2, sectors, multiply_left, 0)
         pl.when(below >= 0)(functools.partial(near_arrived, below))
         pl.when(above < depth)(functools.partial(near_arrived, above))
-    for h in (0, 1):
-        for zz in range(depth):
-            for p in (0, 1):
-                to_far(h, zz, p).wait_recv()
-
-    def swap(s):
-        span = pl.ds(s * coupled, coupled)
-        return remote(
-            part.at[1 - core, span], partner_part.at[span], p_send.at[s], p_recv.at[s], {"op": 1 - core}
-        )
-
-    def multiply_right(s, _):
-        for n in range(coupled):
-            j = s * coupled + n
-            owner = block_right[me * blocks + j] // sectors
-            oz, oy, ox = owner // 4, (owner // 2) % 2, owner % 2
-            slot = rank[j]
-            top = jnp.where(ox == x, full[0, oz, oy, s], got[0, oz, oy, slot])
-            low = jnp.where(oy == y, full[1, oz, ox, s], got[1, oz, ox, slot])
-            env = jnp.concatenate([top, low], axis=0)
-            value = lax.dot_general(
-                products[j], env, (((1,), (1,)), ((), ())), preferred_element_type=jnp.float32
-            )
-            part[0, j] = value[:half].astype(part.dtype)
-            part[1, j] = value[half:].astype(part.dtype)
-        swap(s).start()
-        return 0
-
-    def finish(s):
-        swap(s).wait_recv()
+        if step == 1:
+            multiply_right(z)
+        else:
+            pl.when(below + 1 >= 0)(functools.partial(multiply_right, below + 1))
+            pl.when(above - 1 < depth)(functools.partial(multiply_right, above - 1))
+    pl.when(z - depth + 1 >= 0)(functools.partial(multiply_right, z - depth + 1))
+    pl.when(z + depth - 1 < depth)(functools.partial(multiply_right, z + depth - 1))
+    def finish(s, _):
         rows = lax.broadcasted_iota(jnp.int32, (half, width), 0) + core * half
         row_limit = left_dims[me * sectors + s]
         for n in range(coupled):
             j = s * coupled + n
-            col_limit = right_dims[block_right[me * blocks + j]]
-            value = part[core, j].astype(jnp.float32) + partner_part[j].astype(jnp.float32)
-            keep = (rows < row_limit) & (columns[:half] < col_limit)
+            right = block_right[me * blocks + j]
+            owner = right // sectors
+            oz, i = owner // 4, (owner % 4) * slots + rank[me, j]
+            value = part[core, oz, i] + partner_part[oz, i]
+            keep = (rows < row_limit) & (columns[:half] < right_dims[right])
             out[j] = jnp.where(keep, value, 0.0).astype(jnp.bfloat16)
-
-    lag = 2
-    lax.fori_loop(0, lag, multiply_right, 0)
-
-    def both(s, _):
-        multiply_right(s, 0)
-        finish(s - lag)
         return 0
 
-    lax.fori_loop(lag, sectors, both, 0)
-
-    def last(s, _):
-        finish(s)
-        return 0
-
-    lax.fori_loop(sectors - lag, sectors, last, 0)
-
-    def drain(s, _):
-        swap(s).wait_send()
-        return 0
-
-    lax.fori_loop(0, sectors, drain, 0)
+    for zz in range(depth):
+        swap(zz).wait_recv()
+    lax.fori_loop(0, sectors, finish, 0)
+    for zz in range(depth):
+        swap(zz).wait_send()
     for h in (0, 1):
         for zz in range(depth):
             to_near(h, zz).wait_send()
@@ -259,17 +257,15 @@
 
 
 def tables(block_right, devices, blocks, sectors):
-    me = lax.axis_index("sector")
     slots = blocks // devices
-    members = jnp.stack([me, me ^ 1, me ^ 2])
-    owners = (block_right.reshape(devices, blocks) // sectors)[members]
+    owners = (block_right // sectors).reshape(devices, blocks)
     position = jnp.arange(blocks, dtype=jnp.int32)
     earlier = (owners[:, None, :] == owners[:, :, None]) & (position[None, None, :] < position[None, :, None])
     rank = jnp.sum(earlier.astype(jnp.int32), axis=2)
-    code = owners[1:] * slots + rank[1:]
+    code = owners * slots + rank
     hit = code[:, None, :] == jnp.arange(devices * slots, dtype=jnp.int32)[None, :, None]
-    source = jnp.sum(hit * (position // (blocks // sectors)), axis=2)
-    return rank[0], source.reshape(-1)
+    source = jnp.sum(jnp.where(hit, position, 0), axis=2)
+    return rank, source
 
 
 def per_device(psi, left_env, right_env, left_dims, right_dims, block_right):
@@ -294,8 +290,8 @@
             pltpu.VMEM((2, depth, 2, sectors, half, width), bf16),
             pltpu.VMEM((2, depth, 2, slots, half, width), bf16),
             pltpu.VMEM((2, depth, 2, slots, half, width), bf16),
-            pltpu.VMEM((2, blocks, half, width), jnp.float32),
-            pltpu.VMEM((blocks, half, width), jnp.float32),
+            pltpu.VMEM((2, depth, 4 * slots, half, width), jnp.float32),
+            pltpu.VMEM((depth, 4 * slots, half, width), jnp.float32),
             dma((2,)),
             dma((2,)),
             dma((2, depth, 2)),
@@ -304,8 +300,8 @@
             dma((2, depth)),
             dma((2, depth, 2)),
             dma((2, depth, 2)),
-            dma((sectors,)),
-            dma((sectors,)),
+            dma((depth,)),
+            dma((depth,)),
         ],
         compiler_params=pltpu.CompilerParams(collective_id=0, has_side_effects=True),
     )(block_right, left_dims, right_dims, rank, source, psi, left_env, right_env)

time: 47.8 us -> 46.6 us (0.975)
  local copies, waits for them, and re-layouts: 4.77 us -> 2.34 us
  other arithmetic: 0.44 us -> 2.17 us
  Pallas kernels: 42.3 us -> 41.8 us
    reshape x2 -> x0, local copies, waits for them, and re-layouts: 1.44 us -> none  [the longest x1 0.76 us: tables(): owners = (block_right.reshape(devices, blocks) // sectors)[members]]
    reduce_sum x1, other arithmetic: 0.11 us -> 0.94 us  [tables(): source = jnp.sum(jnp.where(hit, position, 0), axis=2)]
    select_n x3 -> x1, other arithmetic: 0.09 us -> 0.69 us  [tables(): owners = (block_right // sectors).reshape(devices, blocks)]
    gather x1 -> x0, local copies, waits for them, and re-layouts: 0.56 us -> none  [tables(): owners = (block_right.reshape(devices, blocks) // sectors)[members]]
    squeeze x1 -> x0, local copies, waits for them, and re-layouts: 0.52 us -> none  [tables(): return (rank[0], source.reshape(-1))]
    pallas_call x1, Pallas kernels: 42.3 us -> 41.8 us  [per_device(): pl.pallas_call(functools.partial(gather_kernel, devices), out_shape=jax.S...]
    unnamed x1 -> x3, local copies, waits for them, and re-layouts: 2.26 us -> 2.27 us
where the time goes in v2:
time: 46.6 us; the launch traced here: 46.4 us
  Pallas kernels  41.8 us (90%)
  local copies, waits for them, and re-layouts  2.34 us (5%)
  other arithmetic  2.17 us (5%)
    pallas_call x1, Pallas kernels, per_device(): pl.pallas_call(functools.partial(gather_kernel, devices), out_shape=jax.S...  41.8 us
    unnamed x3, local copies, waits for them, and re-layouts  2.27 us
    reduce_sum x1, other arithmetic, tables(): source = jnp.sum(jnp.where(hit, position, 0), axis=2)  0.94 us

profile of v2, /device:TPU:1, one launch (start us, length us, event | category | flops | bytes accessed | tf_op | source)
XLA Modules:
  0.0 46.4 jit_solution(6753448847091580368)
XLA Ops:
  0.0 0.7 %add_select_fusion = s32[1024]{0:T(1024)S(1)} fusion(s32[1024]{0:T(1024)} %block_right.1), kind=kLoop, calls=%fused_computation.5 | loop fusion | flops 15360 | bytes 8192 | tf_op jit(solution)/shard_map/jit(floor_divide)/jit(_where)/select_n | solution.py:261
  0.7 0.1 eq.28
  0.8 0.5 %convert_reduce_fusion.rank = s32[16,64]{1,0:T(8,128)S(1)} fusion(s32[16,64]{1,0:T(8,128)S(1)} %eq.28, pred[64,64]{1,0:T(8,128)(4,1)S(1)} %iota_compare_fusion.1), kind=kLoop, calls=%fused_computation.2 | loop fusion | flops 261120 | bytes 12288 | tf_op jit(solution)/shard_map/reduce_sum | solution.py:264
  1.3 0.0 copy-start
  1.3 0.9 %select_reduce_fusion.source = s32[16,64]{1,0:T(8,128)} fusion(s32[16,64]{1,0:T(8,128)S(1)} %multiply_add_fusion), kind=kLoop, calls=%fused_computation | loop fusion | flops 195584 | bytes 8192 | tf_op jit(solution)/shard_map/reduce_sum | solution.py:267
  2.3 0.0 copy-done
  2.3 41.8 %shard_map.64 = bf16[64,64,128]{2,1,0:T(8,128)(2,1)} custom-call(s32[1024]{0:T(1024)} %block_right.1, s32[128]{0:T(128)} %left_dims.1, s32[128]{0:T(128)} %right_dims.1, s32[16,64]{1,0:T(8,128)} %copy-done, s32[16,64]{1,0:T(8,128)} %select_reduce_fusion.source, bf16[64,128,128]{2,1,0:T(8,128)(2,1)} %psi_hbm.1, bf16[1,8,128,128]{3,2,1,0:T(8,128)(2,1)} %left_hbm.1, ...), custom_call_target="tpu_custom_call" | custom-call | tf_op jit(solution)/shard_map/pallas_call | solution.py:281
  44.1 2.3 %copy.8 = bf16[64,64,128]{2,1,0:T(8,128)(2,1)} copy(bf16[64,64,128]{2,1,0:T(8,128)(2,1)} %shard_map.64) | data formatting | bytes 2097152
  (2 shorter events, 0.0 us)
Async XLA Ops:
  1.3 1.0 %copy-start = (s32[16,64]{1,0:T(8,128)}, s32[16,64]{1,0:T(8,128)S(1)}, u32[]{:S(2)}) copy-start(s32[16,64]{1,0:T(8,128)S(1)} %convert_reduce_fusion.rank) | copy-start | bytes 12292

commit v3 on v2

--- a/solution.py
+++ b/solution.py
@@ -68,8 +68,8 @@
 
 
 def gather_kernel(
-    devices, block_right, left_dims, right_dims, rank, source, psi_hbm, left_hbm, right_hbm, out,
-    psi, left, products, full, stage, got, part, partner_part,
+    devices, block_right, left_dims, right_dims, rank, source, psi_hbm, left_hbm, right_hbm, out_hbm,
+    out, out_sem, psi, left, products, full, stage, got, part, partner_part,
     local_sem, own_sem, z_send, z_recv, n_send, n_recv, s_send, s_recv, p_send, p_recv,
 ):
     me = lax.axis_index("sector")
@@ -119,14 +119,17 @@
             src_ref=src, dst_ref=dst, send_sem=send, recv_sem=recv, device_id=target, device_id_type=MESH
         )
 
-    def along_z(h, zz, up):
-        block = full.at[h, zz, place[h]]
+    pieces = z_recv.shape[2]
+    piece = sectors // pieces
+
+    def along_z(h, zz, q, up):
+        block = full.at[h, zz, place[h], pl.ds(q * piece, piece)]
         target = {"sector": me + 4 if up else me - 4}
-        return remote(block, block, z_send.at[h, zz, int(up)], z_recv.at[h, zz], target)
-
-    def to_near(h, zz):
-        block = full.at[h, zz, place[h]]
-        return remote(block, block, n_send.at[h, zz], n_recv.at[h, zz], {"sector": near[h]})
+        return remote(block, block, z_send.at[h, zz, q, int(up)], z_recv.at[h, zz, q], target)
+
+    def to_near(h, zz, q):
+        block = full.at[h, zz, place[h], pl.ds(q * piece, piece)]
+        return remote(block, block, n_send.at[h, zz, q], n_recv.at[h, zz, q], {"sector": near[h]})
 
     def to_far(h, zz, p):
         return remote(
@@ -143,19 +146,26 @@
             stage[h, zz, p, t] = value
         to_far(h, zz, p).start()
 
-    def arrived(zz, ups):
+    def arrived(zz, ups, wait):
         for h in (0, 1):
-            for up in ups:
-                @pl.when(z < depth - 1 if up else z > 0)
-                def _():
-                    along_z(h, zz, up).start()
-            to_near(h, zz).start()
-        for h in (0, 1):
-            select_and_send(h, zz, place[h])
+            for q in range(pieces):
+                if wait:
+                    along_z(h, zz, q, ups[0]).wait_recv()
+                for up in ups:
+                    @pl.when(z < depth - 1 if up else z > 0)
+                    def _():
+                        along_z(h, zz, q, up).start()
+                to_near(h, zz, q).start()
+            if wait:
+                select_and_send(h, zz, place[h])
+        if not wait:
+            for h in (0, 1):
+                select_and_send(h, zz, place[h])
 
     def near_arrived(zz):
         for h in (0, 1):
-            to_near(h, zz).wait_recv()
+            for q in range(pieces):
+                to_near(h, zz, q).wait_recv()
             select_and_send(h, zz, 1 - place[h])
 
     columns = lax.broadcasted_iota(jnp.int32, (width, width), 1)
@@ -203,7 +213,7 @@
         lax.fori_loop(0, 4 * slots, one, 0, unroll=4)
         swap(zz).start()
 
-    arrived(z, (False, True))
+    arrived(z, (False, True), False)
     load_left.wait()
     load_psi.wait()
     lax.fori_loop(0, sectors // 2, multiply_left, 0)
@@ -212,9 +222,7 @@
         below, above = z - step, z + step
 
         def enter(zz, up):
-            for h in (0, 1):
-                along_z(h, zz, up).wait_recv()
-            arrived(zz, (up,))
+            arrived(zz, (up,), True)
 
         pl.when(below >= 0)(functools.partial(enter, below, True))
         pl.when(above < depth)(functools.partial(enter, above, False))
@@ -240,20 +248,28 @@
             value = part[core, oz, i] + partner_part[oz, i]
             keep = (rows < row_limit) & (columns[:half] < right_dims[right])
             out[j] = jnp.where(keep, value, 0.0).astype(jnp.bfloat16)
+        store(s).start()
         return 0
+
+    def store(s):
+        span = pl.ds(s * coupled, coupled)
+        return pltpu.make_async_copy(out.at[span], out_hbm.at[span], out_sem.at[s])
 
     for zz in range(depth):
         swap(zz).wait_recv()
     lax.fori_loop(0, sectors, finish, 0)
+    for s in range(sectors):
+        store(s).wait()
     for zz in range(depth):
         swap(zz).wait_send()
     for h in (0, 1):
         for zz in range(depth):
-            to_near(h, zz).wait_send()
             for p in (0, 1):
                 to_far(h, zz, p).wait_send()
-            pl.when((z > 0) & (z <= zz))(lambda: along_z(h, zz, False).wait_send())
-            pl.when((z < depth - 1) & (z >= zz))(lambda: along_z(h, zz, True).wait_send())
+            for q in range(pieces):
+                to_near(h, zz, q).wait_send()
+                pl.when((z > 0) & (z <= zz))(lambda: along_z(h, zz, q, False).wait_send())
+                pl.when((z < depth - 1) & (z >= zz))(lambda: along_z(h, zz, q, True).wait_send())
 
 
 def tables(block_right, devices, blocks, sectors):
@@ -275,6 +291,7 @@
     if cores != 2 or devices % 4 or terms != 1 or blocks % devices or blocks // devices > sectors:
         return exchange_path(psi, left_env, right_env, left_dims, right_dims, block_right)
     depth, half, slots = devices // 4, width // 2, blocks // devices
+    pieces = 2 if sectors % 2 == 0 else 1
     rank, source = tables(block_right, devices, blocks, sectors)
     smem, anywhere = pl.BlockSpec(memory_space=pltpu.SMEM), pl.BlockSpec(memory_space=pl.ANY)
     dma, bf16 = pltpu.SemaphoreType.DMA, jnp.bfloat16
@@ -282,8 +299,10 @@
         functools.partial(gather_kernel, devices),
         out_shape=jax.ShapeDtypeStruct((blocks, half, width), bf16),
         in_specs=[smem] * 5 + [anywhere] * 3,
-        out_specs=pl.BlockSpec(memory_space=pltpu.VMEM),
+        out_specs=anywhere,
         scratch_shapes=[
+            pltpu.VMEM((blocks, half, width), bf16),
+            dma((sectors,)),
             pltpu.VMEM((blocks, width, width), bf16),
             pltpu.VMEM((sectors, width, width), bf16),
             pltpu.VMEM((blocks, width, width), bf16),
@@ -294,10 +313,10 @@
             pltpu.VMEM((depth, 4 * slots, half, width), jnp.float32),
             dma((2,)),
             dma((2,)),
-            dma((2, depth, 2)),
-            dma((2, depth)),
-            dma((2, depth)),
-            dma((2, depth)),
+            dma((2, depth, pieces, 2)),
+            dma((2, depth, pieces)),
+            dma((2, depth, pieces)),
+            dma((2, depth, pieces)),
             dma((2, depth, 2)),
             dma((2, depth, 2)),
             dma((depth,)),

time: 46.6 us -> 46 us (0.987)
  Pallas kernels: 41.8 us -> 41.2 us
    pallas_call x1, Pallas kernels: 41.8 us -> 41.2 us  [per_device(): pl.pallas_call(functools.partial(gather_kernel, devices), out_shape=jax.S...]
where the time goes in v3:
time: 46 us; the launch traced here: 45.8 us
  Pallas kernels  41.2 us (90%)
  local copies, waits for them, and re-layouts  2.34 us (5%)
  other arithmetic  2.17 us (5%)
    pallas_call x1, Pallas kernels, per_device(): pl.pallas_call(functools.partial(gather_kernel, devices), out_shape=jax.S...  41.2 us
    unnamed x3, local copies, waits for them, and re-layouts  2.27 us
    reduce_sum x1, other arithmetic, tables(): source = jnp.sum(jnp.where(hit, position, 0), axis=2)  0.94 us

profile of v3, /device:TPU:1, one launch (start us, length us, event | category | flops | bytes accessed | tf_op | source)
XLA Modules:
  0.0 45.8 jit_solution(13503805157134069828)
XLA Ops:
  0.0 0.7 %add_select_fusion = s32[1024]{0:T(1024)S(1)} fusion(s32[1024]{0:T(1024)} %block_right.1), kind=kLoop, calls=%fused_computation.5 | loop fusion | flops 15360 | bytes 8192 | tf_op jit(solution)/shard_map/jit(floor_divide)/jit(_where)/select_n | solution.py:277
  0.7 0.1 eq.28
  0.8 0.5 %convert_reduce_fusion.rank = s32[16,64]{1,0:T(8,128)S(1)} fusion(s32[16,64]{1,0:T(8,128)S(1)} %eq.28, pred[64,64]{1,0:T(8,128)(4,1)S(1)} %iota_compare_fusion.1), kind=kLoop, calls=%fused_computation.2 | loop fusion | flops 261120 | bytes 12288 | tf_op jit(solution)/shard_map/reduce_sum | solution.py:280
  1.3 0.0 copy-start
  1.3 0.9 %select_reduce_fusion.source = s32[16,64]{1,0:T(8,128)} fusion(s32[16,64]{1,0:T(8,128)S(1)} %multiply_add_fusion), kind=kLoop, calls=%fused_computation | loop fusion | flops 195584 | bytes 8192 | tf_op jit(solution)/shard_map/reduce_sum | solution.py:283
  2.3 0.0 copy-done
  2.3 41.2 %shard_map.64 = bf16[64,64,128]{2,1,0:T(8,128)(2,1)} custom-call(s32[1024]{0:T(1024)} %block_right.1, s32[128]{0:T(128)} %left_dims.1, s32[128]{0:T(128)} %right_dims.1, s32[16,64]{1,0:T(8,128)} %copy-done, s32[16,64]{1,0:T(8,128)} %select_reduce_fusion.source, bf16[64,128,128]{2,1,0:T(8,128)(2,1)} %psi_hbm.1, bf16[1,8,128,128]{3,2,1,0:T(8,128)(2,1)} %left_hbm.1, ...), custom_call_target="tpu_custom_call" | custom-call | tf_op jit(solution)/shard_map/pallas_call | solution.py:298
  43.5 2.3 %copy.8 = bf16[64,64,128]{2,1,0:T(8,128)(2,1)} copy(bf16[64,64,128]{2,1,0:T(8,128)(2,1)} %shard_map.64) | data formatting | bytes 2097152
  (2 shorter events, 0.0 us)
Async XLA Ops:
  1.3 1.0 %copy-start = (s32[16,64]{1,0:T(8,128)}, s32[16,64]{1,0:T(8,128)S(1)}, u32[]{:S(2)}) copy-start(s32[16,64]{1,0:T(8,128)S(1)} %convert_reduce_fusion.rank) | copy-start | bytes 12292

commit v4 on v3

--- a/solution.py
+++ b/solution.py
@@ -185,13 +185,15 @@
             part.at[1 - core, zz], partner_part.at[zz], p_send.at[zz], p_recv.at[zz], {"op": 1 - core}
         )
 
-    def pick(h, zz, p, wanted):
+    def pick(h, zz, p, wanted, whole):
+        if whole:
+            return full[h, zz, p, wanted]
         value = full[h, zz, p, 0]
         for s in range(1, sectors):
             value = jnp.where(wanted == s, full[h, zz, p, s], value)
         return value
 
-    def multiply_right(zz):
+    def multiply_right(zz, whole=False):
         for h in (0, 1):
             for p in (0, 1):
                 to_far(h, zz, p).wait_recv()
@@ -200,8 +202,8 @@
             oy, ox, slot = i // (2 * slots), (i // slots) % 2, i % slots
             j = source[me, (zz * 4 + oy * 2 + ox) * slots + slot]
             wanted = j // coupled
-            top = jnp.where(ox == x, pick(0, zz, oy, wanted), got[0, zz, oy, slot])
-            low = jnp.where(oy == y, pick(1, zz, ox, wanted), got[1, zz, ox, slot])
+            top = jnp.where(ox == x, pick(0, zz, oy, wanted, whole), got[0, zz, oy, slot])
+            low = jnp.where(oy == y, pick(1, zz, ox, wanted, whole), got[1, zz, ox, slot])
             env = jnp.concatenate([top, low], axis=0)
             value = lax.dot_general(
                 products[j], env, (((1,), (1,)), ((), ())), preferred_element_type=jnp.float32
@@ -235,8 +237,8 @@
         else:
             pl.when(below + 1 >= 0)(functools.partial(multiply_right, below + 1))
             pl.when(above - 1 < depth)(functools.partial(multiply_right, above - 1))
-    pl.when(z - depth + 1 >= 0)(functools.partial(multiply_right, z - depth + 1))
-    pl.when(z + depth - 1 < depth)(functools.partial(multiply_right, z + depth - 1))
+    pl.when(z - depth + 1 >= 0)(functools.partial(multiply_right, z - depth + 1, True))
+    pl.when(z + depth - 1 < depth)(functools.partial(multiply_right, z + depth - 1, True))
     def finish(s, _):
         rows = lax.broadcasted_iota(jnp.int32, (half, width), 0) + core * half
         row_limit = left_dims[me * sectors + s]

time: 46 us -> 45.8 us (level)
  no operation moved by 1% of the time
where the time goes in v4:
time: 45.8 us; the launch traced here: 45.6 us
  Pallas kernels  41 us (90%)
  local copies, waits for them, and re-layouts  2.34 us (5%)
  other arithmetic  2.17 us (5%)
    pallas_call x1, Pallas kernels, per_device(): pl.pallas_call(functools.partial(gather_kernel, devices), out_shape=jax.S...  41 us
    unnamed x3, local copies, waits for them, and re-layouts  2.27 us
    reduce_sum x1, other arithmetic, tables(): source = jnp.sum(jnp.where(hit, position, 0), axis=2)  0.94 us

profile of v4, /device:TPU:1, one launch (start us, length us, event | category | flops | bytes accessed | tf_op | source)
XLA Modules:
  0.0 45.6 jit_solution(1859107420713809159)
XLA Ops:
  0.0 0.7 %add_select_fusion = s32[1024]{0:T(1024)S(1)} fusion(s32[1024]{0:T(1024)} %block_right.1), kind=kLoop, calls=%fused_computation.5 | loop fusion | flops 15360 | bytes 8192 | tf_op jit(solution)/shard_map/jit(floor_divide)/jit(_where)/select_n | solution.py:279
  0.7 0.1 eq.28
  0.8 0.5 %convert_reduce_fusion.rank = s32[16,64]{1,0:T(8,128)S(1)} fusion(s32[16,64]{1,0:T(8,128)S(1)} %eq.28, pred[64,64]{1,0:T(8,128)(4,1)S(1)} %iota_compare_fusion.1), kind=kLoop, calls=%fused_computation.2 | loop fusion | flops 261120 | bytes 12288 | tf_op jit(solution)/shard_map/reduce_sum | solution.py:282
  1.3 0.0 copy-start
  1.3 0.9 %select_reduce_fusion.source = s32[16,64]{1,0:T(8,128)} fusion(s32[16,64]{1,0:T(8,128)S(1)} %multiply_add_fusion), kind=kLoop, calls=%fused_computation | loop fusion | flops 195584 | bytes 8192 | tf_op jit(solution)/shard_map/reduce_sum | solution.py:285
  2.3 0.0 copy-done
  2.3 41.0 %shard_map.64 = bf16[64,64,128]{2,1,0:T(8,128)(2,1)} custom-call(s32[1024]{0:T(1024)} %block_right.1, s32[128]{0:T(128)} %left_dims.1, s32[128]{0:T(128)} %right_dims.1, s32[16,64]{1,0:T(8,128)} %copy-done, s32[16,64]{1,0:T(8,128)} %select_reduce_fusion.source, bf16[64,128,128]{2,1,0:T(8,128)(2,1)} %psi_hbm.1, bf16[1,8,128,128]{3,2,1,0:T(8,128)(2,1)} %left_hbm.1, ...), custom_call_target="tpu_custom_call" | custom-call | tf_op jit(solution)/shard_map/pallas_call | solution.py:300
  43.3 2.3 %copy.8 = bf16[64,64,128]{2,1,0:T(8,128)(2,1)} copy(bf16[64,64,128]{2,1,0:T(8,128)(2,1)} %shard_map.64) | data formatting | bytes 2097152
  (2 shorter events, 0.0 us)
Async XLA Ops:
  1.3 1.0 %copy-start = (s32[16,64]{1,0:T(8,128)}, s32[16,64]{1,0:T(8,128)S(1)}, u32[]{:S(2)}) copy-start(s32[16,64]{1,0:T(8,128)S(1)} %convert_reduce_fusion.rank) | copy-start | bytes 12292
